TPU v7x, 256 devices: a whole 4x4x8 slice. The times are simulated.
256 devices in a mesh: row: 16 (over z, core), col: 8 (over y_hi, x), depth: 2 (over y_lo).
Axes of the slice: x: 4, y: 4 (y_hi: 2, y_lo: 2; y = y_hi * 2 + y_lo), z: 8, core: 2. Of those that a mesh axis runs over, the one named last changes fastest.
Arguments:
- a_blocks: float32 [32, 32, 256, 256], P('row', ('depth', 'col')), may hold values from -6 to 6
- a_pattern: int32 [32, 32], P('row', ('depth', 'col')), may hold values from 0 to 1, as said below
- b_blocks: float32 [32, 32, 256, 256], P(('depth', 'row'), 'col'), may hold values from -0.125 to 0.125
- b_pattern: int32 [32, 32], P(('depth', 'row'), 'col'), may hold values from 0 to 1, as said below
- c_pattern: int32 [32, 32], P(('row', 'depth'), 'col'), may hold values 0 or 1
Outputs:
- c_blocks: float32 [32, 32, 256, 256], P(('row', 'depth'), 'col')
Inputs may be any that keep to these rules, and one draw needn't show every extreme that they name: Each block row of a_pattern holds between 1 and 8 stored blocks, and some block row holds exactly 8. Each block column of b_pattern holds between 1 and 8 stored blocks, and some block column holds exactly 8.
All inputs are finite; a program needn't handle non-finite values. No bound on the sum of `c_pattern` on one device may be relied on, other than what follows from the above.
Results may differ from a plain program's by a relative error of at most 0.000071.
Values sent between devices are 32-bit elements; how exact they have to be, the bound alone decides.
A program may use at most 128 MiB of HBM per device.

v0:
```python
import jax
import jax.numpy as jnp
from jax import lax
from jax.sharding import PartitionSpec as P


def local(a_blocks, a_pattern, b_blocks, b_pattern, c_pattern):
    left = a_blocks * a_pattern[:, :, None, None].astype(jnp.float32)
    right = b_blocks * b_pattern[:, :, None, None].astype(jnp.float32)
    layer_right = lax.all_gather(right, "row", axis=0, tiled=True)
    partial_value = jnp.einsum(
        "rkab,kcbe->rcae",
        lax.all_gather(left, "col", axis=1, tiled=True),
        layer_right,
        precision=lax.Precision.HIGHEST,
    )
    product = lax.psum_scatter(partial_value, "depth", scatter_dimension=0, tiled=True)
    return product * c_pattern[:, :, None, None].astype(jnp.float32)


def solution(mesh):
    in_specs = (
        P("row", ("depth", "col"), None, None),
        P("row", ("depth", "col")),
        P(("depth", "row"), "col", None, None),
        P(("depth", "row"), "col"),
        P(("row", "depth"), "col"),
    )
    out_specs = P(("row", "depth"), "col", None, None)
    return jax.shard_map(local, mesh=mesh, in_specs=in_specs, out_specs=out_specs, check_vma=False)
```

profile of v0, /device:TPU:1, one launch (start us, length us, event | category | flops | bytes accessed | tf_op | source)
XLA Modules:
  0.0 337.4 jit_solution(12604116690690265737)
XLA Ops:
  6.5 0.0 all-gather.5.cloned.1.call-start
  6.5 0.7 convert_element_type.28
  7.2 2.3 broadcast_multiply_fusion
  9.6 0.0 all-gather.5.cloned.1.call-update
  9.6 0.0 all-gather.3.cloned.1.call-start
  9.6 1.6 copy.8
  11.2 0.7 convert_bitcast_fusion.1
  11.9 1.2 broadcast_multiply_fusion.1
  13.1 0.0 all-gather.3.cloned.1.call-update
  13.1 0.0 copy-start.1
  13.1 0.0 copy-start
  13.1 0.0 all-reduce.3.cloned.1.call-start
  13.2 114.2 %all-gather.5.cloned.1.call-done = f32[2,16,256,256]{3,2,1,0:T(8,128)} async-done(((f32[2,2,256,256]{3,2,1,0:T(8,128)}), f32[2,16,256,256]{3,2,1,0:T(8,128)}) %all-gather.5.cloned.1.call-update) | async-done | bytes 8388624 | tf_op jit(solution)/shard_map/all_gather | solution.py:13
  127.4 96.1 %all-gather.3.cloned.1.call-done = f32[16,4,256,256]{2,3,0,1:T(8,128)} async-done(((f32[1,4,256,256]{2,3,0,1:T(8,128)}), f32[16,4,256,256]{2,3,0,1:T(8,128)}) %all-gather.3.cloned.1.call-update) | async-done | bytes 16777232 | tf_op jit(solution)/shard_map/all_gather | solution.py:10
  223.5 31.1 %fusion.3 = f32[2,4,256,256]{2,3,0,1:T(8,128)} fusion(f32[2,16,256,256]{3,2,1,0:T(8,128)} %all-gather.5.cloned.1.call-done, f32[16,4,256,256]{2,3,0,1:T(8,128)} %all-gather.3.cloned.1.call-done), kind=kOutput, calls=%fused_computation.3 | convolution fusion | flops 25769803776 | bytes 27262976 | tf_op jit(solution)/shard_map/rkab,kcbe->rcae/dot_general | solution.py:11
  254.6 0.0 all-reduce.3.cloned.1.call-update
  254.6 0.0 copy-done.1
  254.6 0.6 dynamic-slice
  255.2 0.0 copy-done
  255.2 72.3 %all-reduce.3.cloned.1.call-done = f32[2,4,256,256]{2,3,0,1:T(8,128)} async-done(((f32[2,4,256,256]{2,3,0,1:T(8,128)}), f32[2,4,256,256]{2,3,0,1:T(8,128)}) %all-reduce.3.cloned.1.call-update) | async-done | bytes 2097168
  327.6 2.0 dynamic-slice_multiply_fusion
  329.6 1.3 copy.9
  (1 shorter events, 0.0 us)
Async XLA Ops:
  6.5 120.8 %all-gather.5.cloned.1.call-start = ((), (), s32[]{:S(2)}) async-start(), calls=%async_computation.1 | async-start | bytes 9437184 | tf_op jit(solution)/shard_map/all_gather | solution.py:13
  9.6 213.9 %all-gather.3.cloned.1.call-start = ((), (), s32[]{:S(2)}) async-start(), calls=%async_computation | async-start | bytes 17825792 | tf_op jit(solution)/shard_map/all_gather | solution.py:10
  13.1 241.5 %copy-start.1 = (u32[256]{0:T(256)S(1)}, u32[256]{0:T(256)}, u32[]{:S(2)}) copy-start(u32[256]{0:T(256)} %constant.7) | copy-start | bytes 3076
  13.1 242.1 %copy-start = (s32[1,4]{1,0:T(1,128)S(1)}, s32[1,4]{1,0:T(1,128)}, u32[]{:S(2)}) copy-start(s32[1,4]{1,0:T(1,128)} %param.9) | copy-start | bytes 52
  13.1 314.4 %all-reduce.3.cloned.1.call-start = ((), (), s32[]{:S(2)}) async-start(), calls=%async_computation.2 | async-start | bytes 4194304
Sparse Core Ops, SparseCore 0:
  10.0 117.3 all-gather.4
  129.2 94.1 all-gather.2
  254.7 72.7 all-reduce.2
where the time goes:
time: 338 us; the launch traced here: 337 us
  waiting for transfers between devices  283 us (84%)
  matrix products  31.1 us (9%)
  between operations  13.2 us (4%)
  other arithmetic  6.93 us (2%)
  local copies, waits for them, and re-layouts  3.46 us (1%)
    all_gather x1, waiting for transfers between devices, local(): lax.all_gather(left, 'col', axis=1, tiled=True)  114 us
    all_gather x1, waiting for transfers between devices, local(): layer_right = lax.all_gather(right, 'row', axis=0, tiled=True)  96.1 us
    unnamed x4, waiting for transfers between devices  72.4 us
    dot_general x1, matrix products, local(): jnp.einsum('rkab,kcbe->rcae', lax.all_gather(left, 'col', axis=1, tiled=T...  31.1 us
  transfers between devices with their start and end apart: 3, of which 3 were waited for; matrix products, arithmetic and copies ran while one was open for 1% of the time, Pallas kernels for 0%

commit v1 on v0

v1 whole, which is shorter than its diff:
```python
import jax
import jax.numpy as jnp
from jax import lax
from jax.experimental import pallas as pl
from jax.experimental.pallas import tpu as pltpu
from jax.sharding import PartitionSpec as P

MESH = pl.DeviceIdType.MESH
BS = 256
SL = 16
CAP = 8
NSLOT = 2 * CAP
NK = 32


def device(row, col, depth):
    return {"row": row, "col": col, "depth": depth}


def sliced(ref, first, count, piece):
    return ref.at[pl.ds(first, count), pl.ds(pl.multiple_of(piece * SL, SL), SL), :]


def gather_transfers(row, col, depth, a2, b2, a3, b3):
    z, core = lax.div(row, 2), lax.rem(row, 2)
    px = lax.rem(col, 4)
    py = lax.div(col, 4) * 2 + depth

    def plane_id(x, y):
        return lax.rem(y, 2) * 8 + lax.div(y, 2) * 4 + x

    def moved(chunk, first, second):
        dx, dy = (first, second) if chunk == 0 else (second, first)
        return lax.rem(px + (dx + 4), 4), lax.rem(py + (dy + 4), 4)

    def plane_device(chunk, first, second):
        x, y = moved(chunk, first, second)
        return device(row, lax.div(y, 2) * 4 + x, lax.rem(y, 2))

    out = []

    def a_piece(chunk, first, second, lo, count):
        if first == 0 and second == 0:
            return a2.at[pl.ds(chunk * CAP + lo, count)]
        return sliced(a3, chunk * CAP + lo, count, plane_id(*moved(chunk, first, second)))

    def a_target(chunk, first, second, lo, count):
        return sliced(a3, chunk * CAP + lo, count, plane_id(*moved(chunk, first, second)))

    half = {1: 0, -1: CAP // 2}
    for chunk in (0, 1):
        for way in (1, -1):
            key = ("A", chunk, 1, way)
            out.append((key, a_piece(chunk, 0, 0, 0, CAP), a_target(chunk, 0, 0, 0, CAP),
                        plane_device(chunk, way, 0), a_target(chunk, -way, 0, 0, CAP), []))
            out.append((("A", chunk, "1h", way), a_piece(chunk, -way, 0, half[way], CAP // 2),
                        a_target(chunk, -way, 0, half[way], CAP // 2), plane_device(chunk, way, 0),
                        a_target(chunk, 2, 0, half[way], CAP // 2), [key]))
        for first in (0, -1, 1, 2):
            needs = {0: [], -1: [("A", chunk, 1, 1)], 1: [("A", chunk, 1, -1)],
                     2: [("A", chunk, "1h", 1), ("A", chunk, "1h", -1)]}[first]
            for way in (1, -1):
                key = ("A", chunk, 2, first, way)
                out.append((key, a_piece(chunk, first, 0, 0, CAP), a_target(chunk, first, 0, 0, CAP),
                            plane_device(chunk, 0, way), a_target(chunk, first, -way, 0, CAP), needs))
                out.append((("A", chunk, "2h", first, way), a_piece(chunk, first, -way, half[way], CAP // 2),
                            a_target(chunk, first, -way, half[way], CAP // 2), plane_device(chunk, 0, way),
                            a_target(chunk, first, 2, half[way], CAP // 2), [key]))

    def b_id(dz, which):
        return lax.rem(z + (dz + 8), 8) * 2 + which

    def b_piece(chunk, dz):
        if dz == 0:
            return b2.at[pl.ds(chunk * CAP, CAP)]
        return sliced(b3, chunk * CAP, CAP, b_id(dz, core))

    def b_target(chunk, dz, which):
        return sliced(b3, chunk * CAP, CAP, b_id(dz, which))

    for chunk in (0, 1):
        arrived = {0: []}
        for way in (1, -1):
            for hop in range(4):
                if hop == 3 and way != (1, -1)[chunk]:
                    continue
                key = ("B", chunk, way, hop)
                out.append((key, b_piece(chunk, -way * hop), b_target(chunk, -way * hop, core),
                            device(b_id(way, core), col, depth), b_target(chunk, -way * (hop + 1), core),
                            [("B", chunk, way, hop - 1)] if hop else []))
                arrived[-way * (hop + 1)] = [key]
        for dz, needs in arrived.items():
            out.append((("S", chunk, dz), b_piece(chunk, dz), b_target(chunk, dz, core),
                        device(z * 2 + 1 - core, col, depth), b_target(chunk, dz, 1 - core), needs))
    return out


def in_level_order(transfers):
    by_key = {t[0]: t for t in transfers}

    def level(key):
        return 1 + max([level(k) for k in by_key[key][5]], default=0)

    return sorted(transfers, key=lambda t: level(t[0]))


NXFER = 70


def exchange_kernel(ap_ref, bp_ref, a_ref, b_ref, a3, b3, pout,
                    a1, b1, pa, pb, my_pa, my_pb, ra, rb, a2, b2,
                    sa, xa, spa, xpa, sb, xb, spb, xpb, own_sem, ring_s, ring_x):
    row, col, depth = lax.axis_index("row"), lax.axis_index("col"), lax.axis_index("depth")
    me_a = depth * 8 + col
    me_b = depth * 16 + row

    def plane(i):
        return device(row, lax.rem(i, 8), lax.div(i, 8))

    def group(i):
        return device(lax.rem(i, 16), col, lax.div(i, 16))

    barrier = pltpu.get_barrier_semaphore()

    @pl.loop(1, 16)
    def _(o):
        pl.semaphore_signal(barrier, inc=1, device_id=plane(lax.rem(me_a + o, 16)), device_id_type=MESH)

    @pl.loop(1, 32)
    def _(o):
        pl.semaphore_signal(barrier, inc=1, device_id=group(lax.rem(me_b + o, 32)), device_id_type=MESH)

    for i in range(2):
        for j in range(2):
            my_pa[i, j] = jnp.full((8, 128), ap_ref[i, j], jnp.int32)
            my_pb[i, j] = jnp.full((8, 128), bp_ref[0, 2 * i + j], jnp.int32)
    pa[me_a] = my_pa[...]
    pb[me_b] = my_pb[depth]
    own_a = pltpu.make_async_copy(a_ref.at[:, :, pl.ds(pl.multiple_of(me_a * SL, SL), SL), :], a1.at[me_a], own_sem.at[0])
    own_b = pltpu.make_async_copy(
        b_ref.at[0, pl.ds(2 * depth, 2), pl.ds(pl.multiple_of(row * SL, SL), SL), :], b1.at[me_b], own_sem.at[1])
    own_a.start()
    own_b.start()
    pl.semaphore_wait(barrier, 46)

    def copy_a(to, frm):
        return pltpu.make_async_remote_copy(
            src_ref=a_ref.at[:, :, pl.ds(pl.multiple_of(to * SL, SL), SL), :], dst_ref=a1.at[frm],
            send_sem=sa.at[to], recv_sem=xa.at[frm], device_id=plane(to), device_id_type=MESH)

    def copy_pa(to, frm):
        return pltpu.make_async_remote_copy(
            src_ref=my_pa, dst_ref=pa.at[frm],
            send_sem=spa.at[to], recv_sem=xpa.at[frm], device_id=plane(to), device_id_type=MESH)

    def copy_b(to, frm):
        return pltpu.make_async_remote_copy(
            src_ref=b_ref.at[0, pl.ds(2 * lax.div(to, 16), 2), pl.ds(pl.multiple_of(lax.rem(to, 16) * SL, SL), SL), :],
            dst_ref=b1.at[frm], send_sem=sb.at[to], recv_sem=xb.at[frm], device_id=group(to), device_id_type=MESH)

    def copy_pb(to, frm):
        return pltpu.make_async_remote_copy(
            src_ref=my_pb.at[lax.div(to, 16)], dst_ref=pb.at[frm],
            send_sem=spb.at[to], recv_sem=xpb.at[frm], device_id=group(to), device_id_type=MESH)

    @pl.loop(1, 32)
    def _(o):
        to = lax.rem(me_b + o, 32)
        copy_pb(to, me_b).start()
        copy_b(to, me_b).start()

    @pl.loop(1, 16)
    def _(o):
        to = lax.rem(me_a + o, 16)
        copy_pa(to, me_a).start()
        copy_a(to, me_a).start()

    @pl.loop(1, 16)
    def _(o):
        frm = lax.rem(me_a + 16 - o, 16)
        copy_pa(frm, frm).wait_recv()
        copy_a(frm, frm).wait_recv()

    own_a.wait()
    lanes = lax.broadcasted_iota(jnp.int32, (8, 128), 1)
    zero = jnp.zeros((8, 128), jnp.int32)

    def rank(ranks, g, k, p, carry):
        before, listed = carry
        ranks[g, k] = jnp.where(p > 0, before, -1)
        return before + p, jnp.where(lanes == k, p, listed)

    def rank_a(s, carry):
        for j in range(2):
            carry = tuple(rank(ra, g, 2 * s + j, pa[s, g, j], carry[g]) for g in range(2))
        return carry

    done = lax.fori_loop(0, 16, rank_a, ((zero, zero), (zero, zero)))
    pout[0] = done[0][1]
    pout[1] = done[1][1]

    def pick(ranks, load, dst, slot):
        g, j = lax.div(slot, CAP), lax.rem(slot, CAP)
        acc = [jnp.zeros((8, 128), jnp.float32)] * 4
        for k in range(NK):
            here = ranks[g, k] == j
            acc = [jnp.where(here, load(g, k, q), acc[q]) for q in range(4)]
        for q in range(4):
            dst[slot, pl.ds(8 * (q // 2), 8), pl.ds(128 * (q % 2), 128)] = acc[q]

    @pl.loop(0, NSLOT)
    def _(slot):
        pick(ra, lambda g, k, q: a1[k // 2, g, k % 2, pl.ds(8 * (q // 2), 8), pl.ds(128 * (q % 2), 128)], a2, slot)

    transfers = in_level_order(gather_transfers(row, col, depth, a2, b2, a3, b3))
    index = {t[0]: i for i, t in enumerate(transfers)}
    made = {}
    for key, src, dst, dev, arrives, needs in transfers:
        i = index[key]
        send = pltpu.make_async_remote_copy(src_ref=src, dst_ref=dst, send_sem=ring_s.at[i], recv_sem=ring_x.at[i],
                                            device_id=dev, device_id_type=MESH)
        recv = pltpu.make_async_remote_copy(src_ref=arrives, dst_ref=arrives, send_sem=ring_s.at[i],
                                            recv_sem=ring_x.at[i], device_id=dev, device_id_type=MESH)
        made[key] = (send, recv)
    arrived = set()

    def start(t):
        for need in t[5]:
            if need not in arrived:
                made[need][1].wait_recv()
                arrived.add(need)
        made[t[0]][0].start()

    put_a = pltpu.make_async_copy(a2, sliced(a3, 0, NSLOT, me_a), own_sem.at[2])
    put_a.start()
    first_a = [t for t in transfers if t[0][0] == "A" and not t[5]]
    for t in first_a:
        start(t)

    @pl.loop(1, 32)
    def _(o):
        frm = lax.rem(me_b + 32 - o, 32)
        copy_pb(frm, frm).wait_recv()
        copy_b(frm, frm).wait_recv()

    own_b.wait()

    def rank_b(k, carry):
        return tuple(rank(rb, g, k, pb[k, g], carry[g]) for g in range(2))

    done = lax.fori_loop(0, NK, rank_b, ((zero, zero), (zero, zero)))
    pout[2] = done[0][1]
    pout[3] = done[1][1]

    @pl.loop(0, NSLOT)
    def _(slot):
        pick(rb, lambda g, k, q: b1[k, g, pl.ds(8 * (q // 2), 8), pl.ds(128 * (q % 2), 128)], b2, slot)

    put_b = pltpu.make_async_copy(b2, sliced(b3, 0, NSLOT, row), own_sem.at[3])
    put_b.start()
    for t in transfers:
        if t not in first_a:
            start(t)
    for t in transfers:
        if t[0] not in arrived:
            made[t[0]][1].wait_recv()
    for t in transfers:
        made[t[0]][0].wait_send()
    put_a.wait()
    put_b.wait()

    @pl.loop(1, 32)
    def _(o):
        to = lax.rem(me_b + o, 32)
        copy_pb(to, me_b).wait_send()
        copy_b(to, me_b).wait_send()

    @pl.loop(1, 16)
    def _(o):
        to = lax.rem(me_a + o, 16)
        copy_pa(to, me_a).wait_send()
        copy_a(to, me_a).wait_send()


def exchange(a_pattern, b_pattern, a_blocks, b_blocks):
    any_spec = pl.BlockSpec(memory_space=pl.ANY)
    smem = pl.BlockSpec(memory_space=pltpu.SMEM)
    dma = pltpu.SemaphoreType.DMA
    f32, i32 = jnp.float32, jnp.int32
    return pl.pallas_call(
        exchange_kernel,
        out_shape=(jax.ShapeDtypeStruct((NSLOT, BS, BS), f32), jax.ShapeDtypeStruct((NSLOT, BS, BS), f32),
                   jax.ShapeDtypeStruct((4, 8, 128), i32)),
        in_specs=[smem, smem, any_spec, any_spec],
        out_specs=(any_spec, any_spec, pl.BlockSpec(memory_space=pltpu.VMEM)),
        scratch_shapes=[
            pltpu.VMEM((16, 2, 2, SL, BS), f32), pltpu.VMEM((NK, 2, SL, BS), f32),
            pltpu.VMEM((16, 2, 2, 8, 128), i32), pltpu.VMEM((NK, 2, 8, 128), i32),
            pltpu.VMEM((2, 2, 8, 128), i32), pltpu.VMEM((2, 2, 8, 128), i32),
            pltpu.VMEM((2, NK, 8, 128), i32), pltpu.VMEM((2, NK, 8, 128), i32),
            pltpu.VMEM((NSLOT, SL, BS), f32), pltpu.VMEM((NSLOT, SL, BS), f32),
            dma((16,)), dma((16,)), dma((16,)), dma((16,)),
            dma((32,)), dma((32,)), dma((32,)), dma((32,)),
            dma((4,)), dma((NXFER,)), dma((NXFER,)),
        ],
        compiler_params=pltpu.CompilerParams(collective_id=0, has_side_effects=True),
        name="exchange",
    )(a_pattern, b_pattern, a_blocks, b_blocks)


def product_kernel(p_ref, a3, b3, out):
    for g in range(2):
        for c in range(2):
            out[g, c] = jnp.zeros((BS, BS), jnp.float32)

            def step(k, carry, g=g, c=c):
                ia, ib = carry
                ha, hb = p_ref[g, 0, k], p_ref[2 + c, 0, k]

                @pl.when(ha * hb > 0)
                def _():
                    out[g, c] += jnp.dot(a3[g * CAP + ia], b3[c * CAP + ib], precision=lax.Precision.HIGHEST,
                                         preferred_element_type=jnp.float32)

                return ia + ha, ib + hb

            lax.fori_loop(0, NK, step, (0, 0))


def product(pout, a3, b3):
    vmem = pl.BlockSpec(memory_space=pltpu.VMEM)
    return pl.pallas_call(
        product_kernel,
        out_shape=jax.ShapeDtypeStruct((2, 2, BS, BS), jnp.float32),
        in_specs=[pl.BlockSpec(memory_space=pltpu.SMEM), vmem, vmem],
        out_specs=vmem,
        name="product",
    )(pout, a3, b3)


def swap_kernel(part, out, sems):
    row, col, depth = lax.axis_index("row"), lax.axis_index("col"), lax.axis_index("depth")
    other = device(row, col, 1 - depth)
    barrier = pltpu.get_barrier_semaphore()
    pl.semaphore_signal(barrier, inc=1, device_id=other, device_id_type=MESH)
    keep = pltpu.make_async_copy(part.at[depth], out.at[pl.ds(2 * depth, 2)], sems.at[0])
    keep.start()
    pl.semaphore_wait(barrier, 1)
    send = pltpu.make_async_remote_copy(src_ref=part.at[1 - depth], dst_ref=out.at[pl.ds(2 * depth, 2)],
                                        send_sem=sems.at[1], recv_sem=sems.at[2], device_id=other, device_id_type=MESH)
    recv = pltpu.make_async_remote_copy(src_ref=part.at[1 - depth], dst_ref=out.at[pl.ds(2 - 2 * depth, 2)],
                                        send_sem=sems.at[1], recv_sem=sems.at[2], device_id=other, device_id_type=MESH)
    send.start()
    keep.wait()
    recv.wait_recv()
    send.wait_send()


def swap(part):
    return pl.pallas_call(
        swap_kernel,
        out_shape=jax.ShapeDtypeStruct((4, BS, BS), jnp.float32),
        in_specs=[pl.BlockSpec(memory_space=pltpu.VMEM)],
        out_specs=pl.BlockSpec(memory_space=pl.ANY),
        scratch_shapes=[pltpu.SemaphoreType.DMA((3,))],
        compiler_params=pltpu.CompilerParams(collective_id=1, has_side_effects=True),
        name="swap",
    )(part)


def local(a_blocks, a_pattern, b_blocks, b_pattern, c_pattern):
    a3, b3, pout = exchange(a_pattern, b_pattern, a_blocks, b_blocks)
    c = swap(product(pout, a3, b3))
    return (c * c_pattern[0][:, None, None].astype(jnp.float32))[None]


def solution(mesh):
    in_specs = (
        P("row", ("depth", "col"), None, None),
        P("row", ("depth", "col")),
        P(("depth", "row"), "col", None, None),
        P(("depth", "row"), "col"),
        P(("row", "depth"), "col"),
    )
    out_specs = P(("row", "depth"), "col", None, None)
    return jax.shard_map(local, mesh=mesh, in_specs=in_specs, out_specs=out_specs, check_vma=False)
```

time: 338 us -> 107 us (0.32)
  waiting for transfers between devices: 283 us -> 0 us
  Pallas kernels: 0 us -> 105 us
  matrix products: 31.1 us -> 0 us
  between operations: 13.2 us -> 0.04 us
  other arithmetic: 6.93 us -> 2.36 us
  local copies, waits for them, and re-layouts: 3.46 us -> 0.01 us
    all_gather x2 -> x0, waiting for transfers between devices: 210 us -> none  [the longest x1 114 us: local(): lax.all_gather(left, 'col', axis=1, tiled=True)]
    pallas_call x0 -> x3, Pallas kernels: none -> 105 us  [the longest x1 81.8 us: exchange(): pl.pallas_call(exchange_kernel, out_shape=(jax.ShapeDtypeStruct((NSLOT, B...]
    unnamed x4 -> x0, waiting for transfers between devices: 72.4 us -> none
    dot_general x1 -> x0, matrix products: 31.1 us -> none  [local(): jnp.einsum('rkab,kcbe->rcae', lax.all_gather(left, 'col', axis=1, tiled=T...]
    mul x3 -> x0, other arithmetic: 5.59 us -> none  [the longest x1 2.35 us: local(): left = a_blocks * a_pattern[:, :, None, None].astype(jnp.float32)]
  transfers between devices with their start and end apart: 3 -> 0, of which waited for: 3 -> 0; matrix products, arithmetic and copies ran while one was open for 1% -> 0% of each run, Pallas kernels for 0% -> 0%
where the time goes in v1:
time: 107 us
  Pallas kernels  105 us (98%)
  other arithmetic  2.36 us (2%)
    pallas_call x1, Pallas kernels, exchange(): pl.pallas_call(exchange_kernel, out_shape=(jax.ShapeDtypeStruct((NSLOT, B...  81.8 us
    pallas_call x1, Pallas kernels, swap(): pl.pallas_call(swap_kernel, out_shape=jax.ShapeDtypeStruct((4, BS, BS), j...  14 us
    pallas_call x1, Pallas kernels, product(): pl.pallas_call(product_kernel, out_shape=jax.ShapeDtypeStruct((2, 2, BS,...  9.01 us
    broadcast_in_dim x1, other arithmetic, local(): return (c * c_pattern[0][:, None, None].astype(jnp.float32))[None]  2.36 us

profile of v1, /device:TPU:1, one launch (start us, length us, event | category | flops | bytes accessed | tf_op | source)
XLA Modules:
  0.0 107.2 jit_solution(10704909007058144417)
XLA Ops:
  0.0 81.8 %exchange.1 = (f32[16,256,256]{2,1,0:T(8,128)}, f32[16,256,256]{2,1,0:T(8,128)}, s32[4,8,128]{2,1,0:T(8,128)}) custom-call(s32[2,2]{1,0:T(2,128)} %ap_ref.1, s32[1,4]{1,0:T(1,128)} %bp_ref.1, f32[2,2,256,256]{3,2,1,0:T(8,128)} %a_ref.1, f32[1,4,256,256]{3,2,1,0:T(8,128)} %b_ref.1), custom_call_target="tpu_custom_call" | custom-call | tf_op jit(solution)/shard_map/exchange/pallas_call | solution.py:290
  81.8 0.0 copy-start
  81.8 9.0 %product.1.part = f32[2,2,256,256]{3,2,1,0:T(8,128)} custom-call(s32[4,8,128]{2,1,0:T(8,128)} %get-tuple-element.8.p_ref, f32[16,256,256]{2,1,0:T(8,128)} %get-tuple-element.9.a3, f32[16,256,256]{2,1,0:T(8,128)} %get-tuple-element.10.b3), custom_call_target="tpu_custom_call" | custom-call | tf_op jit(solution)/shard_map/product/pallas_call | solution.py:332
  90.8 14.0 %swap.1 = f32[4,256,256]{2,1,0:T(8,128)} custom-call(f32[2,2,256,256]{3,2,1,0:T(8,128)} %product.1.part), custom_call_target="tpu_custom_call" | custom-call | tf_op jit(solution)/shard_map/swap/pallas_call | solution.py:360
  104.8 0.0 copy-done
  104.8 2.4 %multiply_bitcast_fusion = f32[1,4,256,256]{3,2,1,0:T(8,128)} fusion(f32[4,256,256]{2,1,0:T(8,128)} %swap.1, f32[4]{0:T(128)S(1)} %convert_bitcast_fusion), kind=kLoop, calls=%fused_computation | loop fusion | flops 262144 | bytes 2097168 | tf_op jit(solution)/shard_map/broadcast_in_dim | solution.py:374
  (1 shorter events, 0.0 us)
Async XLA Ops:
  81.8 23.0 %copy-start = (s32[1,4]{1,0:T(1,128)S(1)}, s32[1,4]{1,0:T(1,128)}, u32[]{:S(2)}) copy-start(s32[1,4]{1,0:T(1,128)} %param.9) | copy-start | bytes 52

commit v2 on v1

v2 whole, which is shorter than its diff:
```python
import jax
import jax.numpy as jnp
from jax import lax
from jax.experimental import pallas as pl
from jax.experimental.pallas import tpu as pltpu
from jax.sharding import PartitionSpec as P

MESH = pl.DeviceIdType.MESH
BS = 256
SL = 16
CAP = 8
NSLOT = 2 * CAP
NK = 32


def device(row, col, depth):
    return {"row": row, "col": col, "depth": depth}


def sliced(ref, first, count, piece):
    return ref.at[pl.ds(first, count), pl.ds(pl.multiple_of(piece * SL, SL), SL), :]


def gather_transfers(row, col, depth, a2, b2, a3, b3):
    z, core = lax.div(row, 2), lax.rem(row, 2)
    px = lax.rem(col, 4)
    py = lax.div(col, 4) * 2 + depth

    def plane_id(x, y):
        return lax.rem(y, 2) * 8 + lax.div(y, 2) * 4 + x

    def moved(chunk, first, second):
        dx, dy = (first, second) if chunk == 0 else (second, first)
        return lax.rem(px + (dx + 4), 4), lax.rem(py + (dy + 4), 4)

    def plane_device(chunk, first, second):
        x, y = moved(chunk, first, second)
        return device(row, lax.div(y, 2) * 4 + x, lax.rem(y, 2))

    out = []

    def a_piece(chunk, first, second, lo, count):
        if first == 0 and second == 0:
            return a2.at[pl.ds(chunk * CAP + lo, count)]
        return sliced(a3, chunk * CAP + lo, count, plane_id(*moved(chunk, first, second)))

    def a_target(chunk, first, second, lo, count):
        return sliced(a3, chunk * CAP + lo, count, plane_id(*moved(chunk, first, second)))

    half = {1: 0, -1: CAP // 2}
    for chunk in (0, 1):
        for way in (1, -1):
            key = ("A", chunk, 1, way)
            out.append((key, a_piece(chunk, 0, 0, 0, CAP), a_target(chunk, 0, 0, 0, CAP),
                        plane_device(chunk, way, 0), a_target(chunk, -way, 0, 0, CAP), []))
            out.append((("A", chunk, "1h", way), a_piece(chunk, -way, 0, half[way], CAP // 2),
                        a_target(chunk, -way, 0, half[way], CAP // 2), plane_device(chunk, way, 0),
                        a_target(chunk, 2, 0, half[way], CAP // 2), [key]))
        for first in (0, -1, 1, 2):
            needs = {0: [], -1: [("A", chunk, 1, 1)], 1: [("A", chunk, 1, -1)],
                     2: [("A", chunk, "1h", 1), ("A", chunk, "1h", -1)]}[first]
            for way in (1, -1):
                key = ("A", chunk, 2, first, way)
                out.append((key, a_piece(chunk, first, 0, 0, CAP), a_target(chunk, first, 0, 0, CAP),
                            plane_device(chunk, 0, way), a_target(chunk, first, -way, 0, CAP), needs))
                out.append((("A", chunk, "2h", first, way), a_piece(chunk, first, -way, half[way], CAP // 2),
                            a_target(chunk, first, -way, half[way], CAP // 2), plane_device(chunk, 0, way),
                            a_target(chunk, first, 2, half[way], CAP // 2), [key]))

    def b_id(dz, which):
        return lax.rem(z + (dz + 8), 8) * 2 + which

    def b_piece(chunk, dz):
        if dz == 0:
            return b2.at[pl.ds(chunk * CAP, CAP)]
        return sliced(b3[chunk], 0, CAP, b_id(dz, core))

    def b_target(chunk, dz, which):
        return sliced(b3[chunk], 0, CAP, b_id(dz, which))

    for chunk in (0, 1):
        arrived = {0: []}
        for way in (1, -1):
            for hop in range(4):
                if hop == 3 and way != (1, -1)[chunk]:
                    continue
                key = ("B", chunk, way, hop)
                out.append((key, b_piece(chunk, -way * hop), b_target(chunk, -way * hop, core),
                            device(b_id(way, core), col, depth), b_target(chunk, -way * (hop + 1), core),
                            [("B", chunk, way, hop - 1)] if hop else []))
                arrived[-way * (hop + 1)] = [key]
        for dz, needs in arrived.items():
            out.append((("S", chunk, dz), b_piece(chunk, dz), b_target(chunk, dz, core),
                        device(z * 2 + 1 - core, col, depth), b_target(chunk, dz, 1 - core), needs))
    return out


NXFER = 70


def start_time(key):
    if key[0] == "A":
        level = {1: 0, "1h": 1}.get(key[2])
        if level is None:
            level = {0: 0, -1: 1, 1: 1, 2: 2}[key[3]] + (1 if key[2] == "2h" else 0)
        return 30 + 6 * level
    first, each = ((24, 4.5), (35, 4.5))[key[1]]
    if key[0] == "B":
        return first + each * key[3]
    return first + each * abs(key[2]) + 0.1


def kernel(ap_ref, bp_ref, a_ref, b_ref, out,
           a1, b1, pa, pb, my_pa, my_pb, ra, rb, a2, b2, a3, b3_0, b3_1, c_own, c_other, match, match_s,
           sa, xa, spa, xpa, sb, xb, spb, xpb, own_sem, ring_s, ring_x, swap_s, swap_x):
    row, col, depth = lax.axis_index("row"), lax.axis_index("col"), lax.axis_index("depth")
    b3 = (b3_0, b3_1)
    me_a = depth * 8 + col
    me_b = depth * 16 + row

    def plane(i):
        return device(row, lax.rem(i, 8), lax.div(i, 8))

    def group(i):
        return device(lax.rem(i, 16), col, lax.div(i, 16))

    def piece(i):
        return pl.ds(pl.multiple_of(i * SL, SL), SL)

    barrier = pltpu.get_barrier_semaphore()

    @pl.loop(1, 16)
    def _(o):
        pl.semaphore_signal(barrier, inc=1, device_id=plane(lax.rem(me_a + o, 16)), device_id_type=MESH)

    @pl.loop(1, 32)
    def _(o):
        pl.semaphore_signal(barrier, inc=1, device_id=group(lax.rem(me_b + o, 32)), device_id_type=MESH)

    for i in range(2):
        for j in range(2):
            my_pa[i, j] = jnp.full((1, 128), ap_ref[i, j], jnp.int32)
            my_pb[i, j] = jnp.full((1, 128), bp_ref[0, 2 * i + j], jnp.int32)
    pa[me_a] = my_pa[...]
    pb[me_b] = my_pb[depth]
    own = [
        pltpu.make_async_copy(a_ref.at[:, :, piece(me_a), :], a1.at[me_a], own_sem.at[0]),
        pltpu.make_async_copy(b_ref.at[0, 2 * depth, piece(row), :], b1.at[0, me_b], own_sem.at[1]),
        pltpu.make_async_copy(b_ref.at[0, 2 * depth + 1, piece(row), :], b1.at[1, me_b], own_sem.at[2]),
    ]
    for copy in own:
        copy.start()
    pl.semaphore_wait(barrier, 46)

    def copy_a(to, frm):
        return pltpu.make_async_remote_copy(
            src_ref=a_ref.at[:, :, piece(to), :], dst_ref=a1.at[frm],
            send_sem=sa.at[to], recv_sem=xa.at[frm], device_id=plane(to), device_id_type=MESH)

    def copy_pa(to, frm):
        return pltpu.make_async_remote_copy(
            src_ref=my_pa, dst_ref=pa.at[frm],
            send_sem=spa.at[to], recv_sem=xpa.at[frm], device_id=plane(to), device_id_type=MESH)

    def copy_b(c, to, frm):
        return pltpu.make_async_remote_copy(
            src_ref=b_ref.at[0, 2 * lax.div(to, 16) + c, piece(lax.rem(to, 16)), :], dst_ref=b1.at[c, frm],
            send_sem=sb.at[c, to], recv_sem=xb.at[c, frm], device_id=group(to), device_id_type=MESH)

    def copy_pb(to, frm):
        return pltpu.make_async_remote_copy(
            src_ref=my_pb.at[lax.div(to, 16)], dst_ref=pb.at[frm],
            send_sem=spb.at[to], recv_sem=xpb.at[frm], device_id=group(to), device_id_type=MESH)

    @pl.loop(1, 32)
    def _(o):
        to = lax.rem(me_b + o, 32)
        copy_pb(to, me_b).start()
        copy_b(0, to, me_b).start()

    @pl.loop(1, 16)
    def _(o):
        to = lax.rem(me_a + o, 16)
        copy_pa(to, me_a).start()
        copy_a(to, me_a).start()

    @pl.loop(1, 32)
    def _(o):
        copy_b(1, lax.rem(me_b + o, 32), me_b).start()

    zero = jnp.zeros((8, 128), jnp.int32)

    def rank(ranks, g, k, p, before):
        p = jnp.broadcast_to(p, (8, 128))
        ranks[g, k] = jnp.where(p > 0, before, -1)
        return before + p

    @pl.loop(1, 32)
    def _(o):
        frm = lax.rem(me_b + 32 - o, 32)
        copy_pb(frm, frm).wait_recv()

    def rank_b(k, carry):
        return tuple(rank(rb, g, k, pb[k, g], carry[g]) for g in range(2))

    lax.fori_loop(0, NK, rank_b, (zero, zero))

    @pl.loop(1, 16)
    def _(o):
        frm = lax.rem(me_a + 16 - o, 16)
        copy_pa(frm, frm).wait_recv()

    def rank_a(s, carry):
        for j in range(2):
            carry = tuple(rank(ra, g, 2 * s + j, pa[s, g, j], carry[g]) for g in range(2))
        return carry

    lax.fori_loop(0, 16, rank_a, (zero, zero))

    lanes = lax.broadcasted_iota(jnp.int32, (8, 128), 1)
    for g in range(2):
        def meet(k, carry, g=g):
            ours = ra[g, k]
            return tuple(jnp.where(lanes == ours, rb[c, k] + 1, carry[c]) for c in range(2))

        met = lax.fori_loop(0, NK, meet, (zero, zero))
        for c in range(2):
            match[g, c] = met[c]

    def pick(ranks, load, dst, slot):
        g, j = lax.div(slot, CAP), lax.rem(slot, CAP)
        acc = [jnp.zeros((8, 128), jnp.float32)] * 4
        for k in range(NK):
            here = ranks[g, k] == j
            acc = [jnp.where(here, load(g, k, q), acc[q]) for q in range(4)]
        for q in range(4):
            dst[slot, pl.ds(8 * (q // 2), 8), pl.ds(128 * (q % 2), 128)] = acc[q]

    def tile(q):
        return pl.ds(8 * (q // 2), 8), pl.ds(128 * (q % 2), 128)

    puts = []

    def pack_a():
        @pl.loop(1, 16)
        def _(o):
            frm = lax.rem(me_a + 16 - o, 16)
            copy_a(frm, frm).wait_recv()

        own[0].wait()

        @pl.loop(0, NSLOT)
        def _(slot):
            pick(ra, lambda g, k, q: a1[(k // 2, g, k % 2, *tile(q))], a2, slot)

        put = pltpu.make_async_copy(a2, sliced(a3, 0, NSLOT, me_a), own_sem.at[3])
        put.start()
        puts.append(put)

    def pack_b(c):
        @pl.loop(1, 32)
        def _(o):
            frm = lax.rem(me_b + 32 - o, 32)
            copy_b(c, frm, frm).wait_recv()

        own[1 + c].wait()

        @pl.loop(c * CAP, (c + 1) * CAP)
        def _(slot):
            pick(rb, lambda g, k, q: b1[(c, k, *tile(q))], b2, slot)

        put = pltpu.make_async_copy(b2.at[pl.ds(c * CAP, CAP)], sliced(b3[c], 0, CAP, row), own_sem.at[4 + c])
        put.start()
        puts.append(put)

    transfers = gather_transfers(row, col, depth, a2, b2, a3, b3)
    assert len(transfers) == NXFER
    made = {}
    for i, (key, src, dst, dev, arrives, needs) in enumerate(transfers):
        made[key] = tuple(
            pltpu.make_async_remote_copy(src_ref=a, dst_ref=b, send_sem=ring_s.at[i], recv_sem=ring_x.at[i],
                                         device_id=dev, device_id_type=MESH)
            for a, b in ((src, dst), (arrives, arrives)))
    arrived = set()

    def wait_for(keys):
        for key in keys:
            if key not in arrived:
                made[key][1].wait_recv()
                arrived.add(key)

    smem_copy = pltpu.make_async_copy(match, match_s, own_sem.at[6])
    smem_copy.start()
    packs = [(23.9, lambda: pack_b(0)), (29.9, pack_a), (34.9, lambda: pack_b(1))]
    for key, src, dst, dev, arrives, needs in sorted(transfers, key=lambda t: start_time(t[0])):
        while packs and packs[0][0] < start_time(key):
            packs.pop(0)[1]()
        wait_for(needs)
        made[key][0].start()

    wait_for([t[0] for t in transfers if t[0][0] == "A"])
    puts[1].wait()
    smem_copy.wait()

    def split(x):
        high = x.astype(jnp.bfloat16)
        return high, (x - high.astype(jnp.float32)).astype(jnp.bfloat16)

    def block(g, c, dst):
        dst[c] = jnp.zeros((BS, BS), jnp.float32)

        @pl.loop(0, CAP)
        def _(j):
            slot = match_s[g, c, 0, j]
            weight = jnp.where(slot > 0, 1.0, 0.0).astype(jnp.float32)
            ah, al = split(a3[g * CAP + j])
            bh, bl = split(b3[c][jnp.maximum(slot - 1, 0)])
            left = jnp.concatenate([ah, ah, al], axis=1)
            right = jnp.concatenate([bh, bl, bh], axis=0)
            dst[c] += weight * jnp.dot(left, right, preferred_element_type=jnp.float32)

    other = device(row, col, 1 - depth)

    def swap(c, d):
        return pltpu.make_async_remote_copy(src_ref=c_other.at[c], dst_ref=out.at[2 * d + c], send_sem=swap_s.at[c],
                                            recv_sem=swap_x.at[c], device_id=other, device_id_type=MESH)

    keeps = []
    for c in range(2):
        wait_for([t[0] for t in transfers if t[0][0] in "BS" and t[0][1] == c])
        puts[2 * c].wait()
        block(1 - depth, c, c_other)
        swap(c, depth).start()
        block(depth, c, c_own)
        keep = pltpu.make_async_copy(c_own.at[c], out.at[2 * depth + c], own_sem.at[7 + c])
        keep.start()
        keeps.append(keep)

    for t in transfers:
        made[t[0]][0].wait_send()

    @pl.loop(1, 32)
    def _(o):
        to = lax.rem(me_b + o, 32)
        copy_pb(to, me_b).wait_send()
        copy_b(0, to, me_b).wait_send()
        copy_b(1, to, me_b).wait_send()

    @pl.loop(1, 16)
    def _(o):
        to = lax.rem(me_a + o, 16)
        copy_pa(to, me_a).wait_send()
        copy_a(to, me_a).wait_send()

    for c in range(2):
        keeps[c].wait()
        swap(c, 1 - depth).wait_recv()
        swap(c, depth).wait_send()


def multiply(a_pattern, b_pattern, a_blocks, b_blocks):
    any_spec = pl.BlockSpec(memory_space=pl.ANY)
    smem = pl.BlockSpec(memory_space=pltpu.SMEM)
    dma = pltpu.SemaphoreType.DMA
    f32, i32 = jnp.float32, jnp.int32
    return pl.pallas_call(
        kernel,
        out_shape=jax.ShapeDtypeStruct((4, BS, BS), f32),
        in_specs=[smem, smem, any_spec, any_spec],
        out_specs=any_spec,
        scratch_shapes=[
            pltpu.VMEM((16, 2, 2, SL, BS), f32), pltpu.VMEM((2, NK, SL, BS), f32),
            pltpu.VMEM((16, 2, 2, 1, 128), i32), pltpu.VMEM((NK, 2, 1, 128), i32),
            pltpu.VMEM((2, 2, 1, 128), i32), pltpu.VMEM((2, 2, 1, 128), i32),
            pltpu.VMEM((2, NK, 8, 128), i32), pltpu.VMEM((2, NK, 8, 128), i32),
            pltpu.VMEM((NSLOT, SL, BS), f32), pltpu.VMEM((NSLOT, SL, BS), f32),
            pltpu.VMEM((NSLOT, BS, BS), f32), pltpu.VMEM((CAP, BS, BS), f32), pltpu.VMEM((CAP, BS, BS), f32),
            pltpu.VMEM((2, BS, BS), f32), pltpu.VMEM((2, BS, BS), f32),
            pltpu.VMEM((2, 2, 8, 128), i32), pltpu.SMEM((2, 2, 8, 128), i32),
            dma((16,)), dma((16,)), dma((16,)), dma((16,)),
            dma((2, 32)), dma((2, 32)), dma((32,)), dma((32,)),
            dma((9,)), dma((NXFER,)), dma((NXFER,)), dma((2,)), dma((2,)),
        ],
        compiler_params=pltpu.CompilerParams(collective_id=0, has_side_effects=True),
        name="multiply",
    )(a_pattern, b_pattern, a_blocks, b_blocks)


def local(a_blocks, a_pattern, b_blocks, b_pattern, c_pattern):
    c = multiply(a_pattern, b_pattern, a_blocks, b_blocks)
    return (c * c_pattern[0][:, None, None].astype(jnp.float32))[None]


def solution(mesh):
    in_specs = (
        P("row", ("depth", "col"), None, None),
        P("row", ("depth", "col")),
        P(("depth", "row"), "col", None, None),
        P(("depth", "row"), "col"),
        P(("row", "depth"), "col"),
    )
    out_specs = P(("row", "depth"), "col", None, None)
    return jax.shard_map(local, mesh=mesh, in_specs=in_specs, out_specs=out_specs, check_vma=False)
```

time: 107 us -> 90.5 us (0.85)
  the two profiles are of different devices: /device:TPU:1 before, /device:TPU:32 now
where the time goes in v2:
time: 90.5 us; the launch traced here: 90.4 us
  Pallas kernels  87.3 us (96%)
  other arithmetic  3.01 us (3%)
    pallas_call x1, Pallas kernels, multiply(): pl.pallas_call(kernel, out_shape=jax.ShapeDtypeStruct((4, BS, BS), f32),...  87.3 us
    broadcast_in_dim x1, other arithmetic, local(): return (c * c_pattern[0][:, None, None].astype(jnp.float32))[None]  2.36 us

profile of v2, /device:TPU:32, one launch (start us, length us, event | category | flops | bytes accessed | tf_op | source)
XLA Modules:
  0.0 90.4 jit_solution(3423238854814993831)
XLA Ops:
  0.0 0.7 convert_bitcast_fusion
  0.7 87.3 %multiply.1 = f32[4,256,256]{2,1,0:T(8,128)} custom-call(s32[2,2]{1,0:T(2,128)} %ap_ref.1, s32[1,4]{1,0:T(1,128)} %bp_ref.1, f32[2,2,256,256]{3,2,1,0:T(8,128)} %a_ref.1, f32[1,4,256,256]{3,2,1,0:T(8,128)} %b_ref.1), custom_call_target="tpu_custom_call" | custom-call | tf_op jit(solution)/shard_map/multiply/pallas_call | solution.py:366
  88.0 2.4 %multiply_bitcast_fusion = f32[1,4,256,256]{3,2,1,0:T(8,128)} fusion(f32[4,256,256]{2,1,0:T(8,128)} %multiply.1, f32[4]{0:T(128)S(1)} %convert_bitcast_fusion), kind=kLoop, calls=%fused_computation | loop fusion | flops 262144 | bytes 2097168 | tf_op jit(solution)/shard_map/broadcast_in_dim | solution.py:391

commit v3 on v2

--- a/solution.py
+++ b/solution.py
@@ -1,3 +1,5 @@
+import functools
+
 import jax
 import jax.numpy as jnp
 from jax import lax
@@ -11,6 +13,9 @@
 CAP = 8
 NSLOT = 2 * CAP
 NK = 32
+A_CHUNKS = ((0, 8, "yx"), (8, 8, "xy"))
+B_CHUNKS = ((0, 0, 4, 1), (0, 4, 4, -1), (1, 0, 4, 1), (1, 4, 4, -1))
+NXFER = 20 * len(A_CHUNKS) + 15 * len(B_CHUNKS)
 
 
 def device(row, col, depth):
@@ -30,7 +35,7 @@
         return lax.rem(y, 2) * 8 + lax.div(y, 2) * 4 + x
 
     def moved(chunk, first, second):
-        dx, dy = (first, second) if chunk == 0 else (second, first)
+        dx, dy = (first, second) if A_CHUNKS[chunk][2] == "xy" else (second, first)
         return lax.rem(px + (dx + 4), 4), lax.rem(py + (dy + 4), 4)
 
     def plane_device(chunk, first, second):
@@ -41,48 +46,51 @@
 
     def a_piece(chunk, first, second, lo, count):
         if first == 0 and second == 0:
-            return a2.at[pl.ds(chunk * CAP + lo, count)]
-        return sliced(a3, chunk * CAP + lo, count, plane_id(*moved(chunk, first, second)))
+            return a2.at[pl.ds(lo, count)]
+        return sliced(a3, lo, count, plane_id(*moved(chunk, first, second)))
 
     def a_target(chunk, first, second, lo, count):
-        return sliced(a3, chunk * CAP + lo, count, plane_id(*moved(chunk, first, second)))
-
-    half = {1: 0, -1: CAP // 2}
-    for chunk in (0, 1):
+        return sliced(a3, lo, count, plane_id(*moved(chunk, first, second)))
+
+    for chunk in range(len(A_CHUNKS)):
+        lo, count, _ = A_CHUNKS[chunk]
+        half = {1: lo, -1: lo + count // 2}
         for way in (1, -1):
             key = ("A", chunk, 1, way)
-            out.append((key, a_piece(chunk, 0, 0, 0, CAP), a_target(chunk, 0, 0, 0, CAP),
-                        plane_device(chunk, way, 0), a_target(chunk, -way, 0, 0, CAP), []))
-            out.append((("A", chunk, "1h", way), a_piece(chunk, -way, 0, half[way], CAP // 2),
-                        a_target(chunk, -way, 0, half[way], CAP // 2), plane_device(chunk, way, 0),
-                        a_target(chunk, 2, 0, half[way], CAP // 2), [key]))
+            out.append((key, a_piece(chunk, 0, 0, lo, count), a_target(chunk, 0, 0, lo, count),
+                        plane_device(chunk, way, 0), a_target(chunk, -way, 0, lo, count), []))
+            out.append((("A", chunk, "1h", way), a_piece(chunk, -way, 0, half[way], count // 2),
+                        a_target(chunk, -way, 0, half[way], count // 2), plane_device(chunk, way, 0),
+                        a_target(chunk, 2, 0, half[way], count // 2), [key]))
         for first in (0, -1, 1, 2):
             needs = {0: [], -1: [("A", chunk, 1, 1)], 1: [("A", chunk, 1, -1)],
                      2: [("A", chunk, "1h", 1), ("A", chunk, "1h", -1)]}[first]
             for way in (1, -1):
                 key = ("A", chunk, 2, first, way)
-                out.append((key, a_piece(chunk, first, 0, 0, CAP), a_target(chunk, first, 0, 0, CAP),
-                            plane_device(chunk, 0, way), a_target(chunk, first, -way, 0, CAP), needs))
-                out.append((("A", chunk, "2h", first, way), a_piece(chunk, first, -way, half[way], CAP // 2),
-                            a_target(chunk, first, -way, half[way], CAP // 2), plane_device(chunk, 0, way),
-                            a_target(chunk, first, 2, half[way], CAP // 2), [key]))
+                out.append((key, a_piece(chunk, first, 0, lo, count), a_target(chunk, first, 0, lo, count),
+                            plane_device(chunk, 0, way), a_target(chunk, first, -way, lo, count), needs))
+                out.append((("A", chunk, "2h", first, way), a_piece(chunk, first, -way, half[way], count // 2),
+                            a_target(chunk, first, -way, half[way], count // 2), plane_device(chunk, 0, way),
+                            a_target(chunk, first, 2, half[way], count // 2), [key]))
 
     def b_id(dz, which):
         return lax.rem(z + (dz + 8), 8) * 2 + which
 
     def b_piece(chunk, dz):
+        c, lo, count, _ = B_CHUNKS[chunk]
         if dz == 0:
-            return b2.at[pl.ds(chunk * CAP, CAP)]
-        return sliced(b3[chunk], 0, CAP, b_id(dz, core))
+            return b2.at[pl.ds(c * CAP + lo, count)]
+        return sliced(b3[c], lo, count, b_id(dz, core))
 
     def b_target(chunk, dz, which):
-        return sliced(b3[chunk], 0, CAP, b_id(dz, which))
-
-    for chunk in (0, 1):
+        c, lo, count, _ = B_CHUNKS[chunk]
+        return sliced(b3[c], lo, count, b_id(dz, which))
+
+    for chunk in range(len(B_CHUNKS)):
         arrived = {0: []}
         for way in (1, -1):
             for hop in range(4):
-                if hop == 3 and way != (1, -1)[chunk]:
+                if hop == 3 and way != B_CHUNKS[chunk][3]:
                     continue
                 key = ("B", chunk, way, hop)
                 out.append((key, b_piece(chunk, -way * hop), b_target(chunk, -way * hop, core),
@@ -95,19 +103,17 @@
     return out
 
 
-NXFER = 70
-
-
 def start_time(key):
     if key[0] == "A":
         level = {1: 0, "1h": 1}.get(key[2])
         if level is None:
             level = {0: 0, -1: 1, 1: 1, 2: 2}[key[3]] + (1 if key[2] == "2h" else 0)
-        return 30 + 6 * level
-    first, each = ((24, 4.5), (35, 4.5))[key[1]]
+        return 38.5 + 0.3 * key[1] + 8.6 * level
+    c, lo = B_CHUNKS[key[1]][:2]
+    times = ((36, 42.6, 49.2, 55.8), (45, 49.8, 54.6, 59.4))[c]
     if key[0] == "B":
-        return first + each * key[3]
-    return first + each * abs(key[2]) + 0.1
+        return times[key[3]] + 1.3 * lo / 4
+    return times[min(abs(key[2]), 3)] + 1.3 * lo / 4 + (0.1 if abs(key[2]) < 4 else 4.5)
 
 
 def kernel(ap_ref, bp_ref, a_ref, b_ref, out,
@@ -239,7 +245,7 @@
     def tile(q):
         return pl.ds(8 * (q // 2), 8), pl.ds(128 * (q % 2), 128)
 
-    puts = []
+    puts = {}
 
     def pack_a():
         @pl.loop(1, 16)
@@ -255,7 +261,7 @@
 
         put = pltpu.make_async_copy(a2, sliced(a3, 0, NSLOT, me_a), own_sem.at[3])
         put.start()
-        puts.append(put)
+        puts[1] = put
 
     def pack_b(c):
         @pl.loop(1, 32)
@@ -271,7 +277,7 @@
 
         put = pltpu.make_async_copy(b2.at[pl.ds(c * CAP, CAP)], sliced(b3[c], 0, CAP, row), own_sem.at[4 + c])
         put.start()
-        puts.append(put)
+        puts[2 * c] = put
 
     transfers = gather_transfers(row, col, depth, a2, b2, a3, b3)
     assert len(transfers) == NXFER
@@ -291,17 +297,6 @@
 
     smem_copy = pltpu.make_async_copy(match, match_s, own_sem.at[6])
     smem_copy.start()
-    packs = [(23.9, lambda: pack_b(0)), (29.9, pack_a), (34.9, lambda: pack_b(1))]
-    for key, src, dst, dev, arrives, needs in sorted(transfers, key=lambda t: start_time(t[0])):
-        while packs and packs[0][0] < start_time(key):
-            packs.pop(0)[1]()
-        wait_for(needs)
-        made[key][0].start()
-
-    wait_for([t[0] for t in transfers if t[0][0] == "A"])
-    puts[1].wait()
-    smem_copy.wait()
-
     def split(x):
         high = x.astype(jnp.bfloat16)
         return high, (x - high.astype(jnp.float32)).astype(jnp.bfloat16)
@@ -326,15 +321,34 @@
                                             recv_sem=swap_x.at[c], device_id=other, device_id_type=MESH)
 
     keeps = []
-    for c in range(2):
-        wait_for([t[0] for t in transfers if t[0][0] in "BS" and t[0][1] == c])
+
+    def start(t):
+        wait_for(t[5])
+        made[t[0]][0].start()
+
+    def column_other(c):
+        wait_for([t[0] for t in transfers if t[0][0] == "A" or B_CHUNKS[t[0][1]][0] == c])
+        if c == 0:
+            puts[1].wait()
+            smem_copy.wait()
         puts[2 * c].wait()
         block(1 - depth, c, c_other)
         swap(c, depth).start()
+
+    def column_own(c):
         block(depth, c, c_own)
         keep = pltpu.make_async_copy(c_own.at[c], out.at[2 * depth + c], own_sem.at[7 + c])
         keep.start()
         keeps.append(keep)
+
+    actions = [(start_time(t[0]), functools.partial(start, t)) for t in transfers]
+    actions += [
+        (35.9, lambda: pack_b(0)), (38.4, pack_a), (44.9, lambda: pack_b(1)),
+        (65.4, lambda: column_other(0)), (68.4, lambda: column_own(0)),
+        (100, lambda: column_other(1)), (101, lambda: column_own(1)),
+    ]
+    for _, action in sorted(actions, key=lambda t: t[0]):
+        action()
 
     for t in transfers:
         made[t[0]][0].wait_send()

time: 90.5 us -> 85.6 us (0.946)
  the two profiles are of different devices: /device:TPU:32 before, /device:TPU:1 now
where the time goes in v3:
time: 85.6 us; the launch traced here: 83.9 us
  Pallas kernels  80.9 us (95%)
  other arithmetic  3.01 us (4%)
    pallas_call x1, Pallas kernels, multiply(): pl.pallas_call(kernel, out_shape=jax.ShapeDtypeStruct((4, BS, BS), f32),...  80.9 us
    broadcast_in_dim x1, other arithmetic, local(): return (c * c_pattern[0][:, None, None].astype(jnp.float32))[None]  2.36 us

profile of v3, /device:TPU:1, one launch (start us, length us, event | category | flops | bytes accessed | tf_op | source)
XLA Modules:
  0.0 83.9 jit_solution(18241774723343617833)
XLA Ops:
  0.0 0.7 convert_bitcast_fusion
  0.7 80.9 %multiply.1 = f32[4,256,256]{2,1,0:T(8,128)} custom-call(s32[2,2]{1,0:T(2,128)} %ap_ref.1, s32[1,4]{1,0:T(1,128)} %bp_ref.1, f32[2,2,256,256]{3,2,1,0:T(8,128)} %a_ref.1, f32[1,4,256,256]{3,2,1,0:T(8,128)} %b_ref.1), custom_call_target="tpu_custom_call" | custom-call | tf_op jit(solution)/shard_map/multiply/pallas_call | solution.py:380
  81.6 2.4 %multiply_bitcast_fusion = f32[1,4,256,256]{3,2,1,0:T(8,128)} fusion(f32[4,256,256]{2,1,0:T(8,128)} %multiply.1, f32[4]{0:T(128)S(1)} %convert_bitcast_fusion), kind=kLoop, calls=%fused_computation | loop fusion | flops 262144 | bytes 2097168 | tf_op jit(solution)/shard_map/broadcast_in_dim | solution.py:405

commit v4 on v3

--- a/solution.py
+++ b/solution.py
@@ -108,9 +108,9 @@
         level = {1: 0, "1h": 1}.get(key[2])
         if level is None:
             level = {0: 0, -1: 1, 1: 1, 2: 2}[key[3]] + (1 if key[2] == "2h" else 0)
-        return 38.5 + 0.3 * key[1] + 8.6 * level
+        return (39.6, 46.3, 54.8, 66.5)[level] + 0.3 * key[1]
     c, lo = B_CHUNKS[key[1]][:2]
-    times = ((36, 42.6, 49.2, 55.8), (45, 49.8, 54.6, 59.4))[c]
+    times = ((36.8, 43.4, 49.2, 55.6), (44.1, 50.2, 54.7, 64.8))[c]
     if key[0] == "B":
         return times[key[3]] + 1.3 * lo / 4
     return times[min(abs(key[2]), 3)] + 1.3 * lo / 4 + (0.1 if abs(key[2]) < 4 else 4.5)
@@ -178,11 +178,24 @@
             src_ref=my_pb.at[lax.div(to, 16)], dst_ref=pb.at[frm],
             send_sem=spb.at[to], recv_sem=xpb.at[frm], device_id=group(to), device_id_type=MESH)
 
-    @pl.loop(1, 32)
-    def _(o):
-        to = lax.rem(me_b + o, 32)
+    def far_first(t):
+        step = lax.div(t + 1, 2)
+        return 8 + step * (2 * lax.rem(t, 2) - 1)
+
+    def each_b(send):
+        @pl.loop(0, 15)
+        def _(t):
+            there = lax.rem(row + far_first(t), 16)
+            send((1 - depth) * 16 + there)
+            send(depth * 16 + there)
+
+        send((1 - depth) * 16 + row)
+
+    def send_first(to):
         copy_pb(to, me_b).start()
         copy_b(0, to, me_b).start()
+
+    each_b(send_first)
 
     @pl.loop(1, 16)
     def _(o):
@@ -190,9 +203,7 @@
         copy_pa(to, me_a).start()
         copy_a(to, me_a).start()
 
-    @pl.loop(1, 32)
-    def _(o):
-        copy_b(1, lax.rem(me_b + o, 32), me_b).start()
+    each_b(lambda to: copy_b(1, to, me_b).start())
 
     zero = jnp.zeros((8, 128), jnp.int32)
 
@@ -343,8 +354,8 @@
 
     actions = [(start_time(t[0]), functools.partial(start, t)) for t in transfers]
     actions += [
-        (35.9, lambda: pack_b(0)), (38.4, pack_a), (44.9, lambda: pack_b(1)),
-        (65.4, lambda: column_other(0)), (68.4, lambda: column_own(0)),
+        (36.66, lambda: pack_b(0)), (39.51, pack_a), (43.97, lambda: pack_b(1)),
+        (70.4, lambda: column_other(0)), (73.4, lambda: column_own(0)),
         (100, lambda: column_other(1)), (101, lambda: column_own(1)),
     ]
     for _, action in sorted(actions, key=lambda t: t[0]):

time: 85.6 us -> 82.5 us (0.964)
  Pallas kernels: 80.9 us -> 78.6 us
    pallas_call x1, Pallas kernels: 80.9 us -> 78.6 us  [multiply(): pl.pallas_call(kernel, out_shape=jax.ShapeDtypeStruct((4, BS, BS), f32),...]
where the time goes in v4:
time: 82.5 us; the launch traced here: 81.7 us
  Pallas kernels  78.6 us (95%)
  other arithmetic  3.01 us (4%)
    pallas_call x1, Pallas kernels, multiply(): pl.pallas_call(kernel, out_shape=jax.ShapeDtypeStruct((4, BS, BS), f32),...  78.6 us
    broadcast_in_dim x1, other arithmetic, local(): return (c * c_pattern[0][:, None, None].astype(jnp.float32))[None]  2.36 us

profile of v4, /device:TPU:1, one launch (start us, length us, event | category | flops | bytes accessed | tf_op | source)
XLA Modules:
  0.0 81.7 jit_solution(9986028421624888295)
XLA Ops:
  0.0 0.7 convert_bitcast_fusion
  0.7 78.6 %multiply.1 = f32[4,256,256]{2,1,0:T(8,128)} custom-call(s32[2,2]{1,0:T(2,128)} %ap_ref.1, s32[1,4]{1,0:T(1,128)} %bp_ref.1, f32[2,2,256,256]{3,2,1,0:T(8,128)} %a_ref.1, f32[1,4,256,256]{3,2,1,0:T(8,128)} %b_ref.1), custom_call_target="tpu_custom_call" | custom-call | tf_op jit(solution)/shard_map/multiply/pallas_call | solution.py:391
  79.3 2.4 %multiply_bitcast_fusion = f32[1,4,256,256]{3,2,1,0:T(8,128)} fusion(f32[4,256,256]{2,1,0:T(8,128)} %multiply.1, f32[4]{0:T(128)S(1)} %convert_bitcast_fusion), kind=kLoop, calls=%fused_computation | loop fusion | flops 262144 | bytes 2097168 | tf_op jit(solution)/shard_map/broadcast_in_dim | solution.py:416

commit v5 on v4

--- a/solution.py
+++ b/solution.py
@@ -14,7 +14,7 @@
 NSLOT = 2 * CAP
 NK = 32
 A_CHUNKS = ((0, 8, "yx"), (8, 8, "xy"))
-B_CHUNKS = ((0, 0, 4, 1), (0, 4, 4, -1), (1, 0, 4, 1), (1, 4, 4, -1))
+B_CHUNKS = ((0, 0, 4, 1), (0, 4, 4, -1), (1, 0, 4, -1), (1, 4, 4, 1))
 NXFER = 20 * len(A_CHUNKS) + 15 * len(B_CHUNKS)
 
 

time: 82.5 us -> 82.5 us (level)
  no operation moved by 1% of the time
where the time goes in v5:
time: 82.5 us; the launch traced here: 81.6 us
  Pallas kernels  78.6 us (95%)
  other arithmetic  3.01 us (4%)
    pallas_call x1, Pallas kernels, multiply(): pl.pallas_call(kernel, out_shape=jax.ShapeDtypeStruct((4, BS, BS), f32),...  78.6 us
    broadcast_in_dim x1, other arithmetic, local(): return (c * c_pattern[0][:, None, None].astype(jnp.float32))[None]  2.36 us

profile of v5, /device:TPU:1, one launch (start us, length us, event | category | flops | bytes accessed | tf_op | source)
XLA Modules:
  0.0 81.6 jit_solution(11206891054455066271)
XLA Ops:
  0.0 0.7 convert_bitcast_fusion
  0.7 78.6 %multiply.1 = f32[4,256,256]{2,1,0:T(8,128)} custom-call(s32[2,2]{1,0:T(2,128)} %ap_ref.1, s32[1,4]{1,0:T(1,128)} %bp_ref.1, f32[2,2,256,256]{3,2,1,0:T(8,128)} %a_ref.1, f32[1,4,256,256]{3,2,1,0:T(8,128)} %b_ref.1), custom_call_target="tpu_custom_call" | custom-call | tf_op jit(solution)/shard_map/multiply/pallas_call | solution.py:391
  79.2 2.4 %multiply_bitcast_fusion = f32[1,4,256,256]{3,2,1,0:T(8,128)} fusion(f32[4,256,256]{2,1,0:T(8,128)} %multiply.1, f32[4]{0:T(128)S(1)} %convert_bitcast_fusion), kind=kLoop, calls=%fused_computation | loop fusion | flops 262144 | bytes 2097168 | tf_op jit(solution)/shard_map/broadcast_in_dim | solution.py:416
